TPU v7x, 32 devices: a whole 2x2x4 slice. The times are simulated.
32 devices in a mesh: tm: 4 (over y, core), space: 8 (over z, x).
Axes of the slice: x: 2, y: 2, z: 4, core: 2. Of those that a mesh axis runs over, the one named last changes fastest.
Arguments:
- state_guess: float32 [8, 16, 96, 128], P('tm', 'space'), may hold values from -6 to 6
- adjoint_guess: float32 [8, 16, 96, 128], P('tm', 'space'), may hold values from -6 to 6
- target: float32 [8, 16, 96, 128], P('tm', 'space'), may hold values from -6 to 6
- initial_state: float32 [16, 96, 128], P('space'), may hold values from -6 to 6
- diffusivity: float32 [16, 96, 128], P('space'), may hold values from 0.3 to 3
Outputs:
- state_field: float32 [8, 16, 96, 128], P('tm', 'space')
- adjoint_field: float32 [8, 16, 96, 128], P('tm', 'space')
All inputs are finite; a program needn't handle non-finite values.
Results may differ from a plain program's by a relative error of at most 0.00025.
Values sent between devices are 32-bit elements; how exact they have to be, the bound alone decides.
A program may use at most 64 MiB of HBM per device.

v0:
```python
import math

import jax
import jax.numpy as jnp
from jax import lax
from jax.sharding import PartitionSpec as P

SWEEPS = 4
OUTER = 2


step_size = 0.25
control_cost = 0.05


def swapped(block, axis, distance):
    count = lax.axis_size(axis)
    route = []
    for low in range(count):
        high = low | 1 << distance
        if high != low and high < count:
            route += [(low, high), (high, low)]
    return lax.ppermute(block, axis, route)


def extended(cells, sides, width):
    for axis, dim in sides:
        count = lax.axis_size(axis)
        ends = count - 1
        head = lax.slice_in_dim(cells, 0, width, axis=dim)
        tail = lax.slice_in_dim(cells, cells.shape[dim] - width, cells.shape[dim], axis=dim)
        cells = jnp.concatenate(
            [
                lax.ppermute(tail, axis, [(i, (i + 1) % count) for i in range(ends)]),
                cells,
                lax.ppermute(head, axis, [((i + 1) % count, i) for i in range(ends)]),
            ],
            axis=dim,
        )
    return cells


def rim_slices(padded):
    return [
        padded[..., 2:, 1:-1, 1:-1],
        padded[..., :-2, 1:-1, 1:-1],
        padded[..., 1:-1, 2:, 1:-1],
        padded[..., 1:-1, :-2, 1:-1],
        padded[..., 1:-1, 1:-1, 2:],
        padded[..., 1:-1, 1:-1, :-2],
    ]


def pad_inner(values):
    widths = [(0, 0)] * (values.ndim - 2) + [(1, 1)] * 2
    return jnp.pad(values, widths)


def neighbour_sum(rimmed, weights):
    pieces = rim_slices(pad_inner(rimmed))
    summed = weights[0] * pieces[0]
    for weight_one, piece_one in zip(weights[1:], pieces[1:]):
        summed = summed + weight_one * piece_one
    return summed


def block_solve(right_side, shift_real, shift_imag, determinant):
    coupling = step_size / control_cost
    state_real = right_side[0]
    state_imag = right_side[1]
    adjoint_real = right_side[2]
    adjoint_imag = right_side[3]
    return jnp.stack(
        [
            (shift_real * state_real + shift_imag * state_imag - coupling * adjoint_real)
            / determinant,
            (shift_real * state_imag - shift_imag * state_real - coupling * adjoint_imag)
            / determinant,
            (step_size * state_real + shift_real * adjoint_real - shift_imag * adjoint_imag)
            / determinant,
            (step_size * state_imag + shift_real * adjoint_imag + shift_imag * adjoint_real)
            / determinant,
        ]
    )


def twiddle(packed, cos_part, sin_part):
    return jnp.stack(
        [
            packed[0] * cos_part - packed[1] * sin_part,
            packed[0] * sin_part + packed[1] * cos_part,
            packed[2] * cos_part - packed[3] * sin_part,
            packed[2] * sin_part + packed[3] * cos_part,
        ]
    )


def butterfly_segment(packed, bit_number, position, device, local_steps, horizon, inverse):
    half_span = local_steps << bit_number
    partner = swapped(packed, "tm", bit_number)
    upper_half = jnp.bitwise_and(jnp.right_shift(device, bit_number), 1) == 0
    offset = jnp.remainder(position, half_span) * (horizon // (2 * half_span))
    angles = (2.0 * math.pi / horizon * offset.astype(jnp.float32)).reshape(-1, 1, 1, 1)
    cos_part = jnp.cos(angles)
    sin_part = jnp.sin(angles)
    if inverse:
        return jnp.where(
            upper_half,
            0.5 * (packed + twiddle(partner, cos_part, sin_part)),
            0.5 * (partner - twiddle(packed, cos_part, sin_part)),
        )
    return jnp.where(upper_half, packed + partner, twiddle(partner - packed, cos_part, -sin_part))


def on_device(state_guess, adjoint_guess, target, initial_state, diffusivity):
    local_steps = state_guess.shape[0]
    section_count = lax.axis_size("tm")
    horizon = local_steps * section_count
    bit_count = horizon.bit_length() - 1
    device = lax.axis_index("tm")
    position = device * local_steps + jnp.arange(local_steps, dtype=jnp.int32)
    kappa_rim = extended(diffusivity, (("space", 0),), 1)
    weights = [0.5 * (diffusivity + beside) for beside in rim_slices(pad_inner(kappa_rim))]
    diagonal = weights[0] + weights[1] + weights[2] + weights[3] + weights[4] + weights[5]
    mode_index = jnp.zeros_like(position)
    for bit_number in range(bit_count):
        picked = jnp.bitwise_and(jnp.right_shift(position, bit_number), 1)
        mode_index = mode_index + jnp.left_shift(picked, bit_count - 1 - bit_number)
    angles = (2.0 * math.pi / horizon * mode_index.astype(jnp.float32)).reshape(-1, 1, 1, 1)
    shift_real = 1.0 - jnp.cos(angles) + step_size * diagonal
    shift_imag = jnp.sin(angles)
    determinant = (
        shift_real * shift_real + shift_imag * shift_imag + step_size * step_size / control_cost
    )
    first_step = jnp.where(device == 0, initial_state, jnp.zeros_like(initial_state))
    source = jnp.concatenate([first_step[None], jnp.zeros_like(state_guess[1:])], 0)
    state_now = state_guess
    adjoint_now = adjoint_guess
    for outer_step in range(OUTER):
        coupled = jnp.stack([state_now, adjoint_now])
        rimmed = extended(coupled, (("tm", 1), ("space", 2)), 1)
        spread_sum = neighbour_sum(rimmed[:, 1:-1], weights)
        before = rimmed[0, :-2, 1:-1]
        later_adjoint = rimmed[1, 2:, 1:-1]
        diffuse_state = diagonal * state_now - spread_sum[0]
        diffuse_adjoint = diagonal * adjoint_now - spread_sum[1]
        res_state = source - (
            state_now - before + step_size * diffuse_state + step_size / control_cost * adjoint_now
        )
        res_adjoint = -step_size * target - (
            adjoint_now - later_adjoint + step_size * diffuse_adjoint - step_size * state_now
        )
        zeros_field = jnp.zeros_like(res_state)
        packed = jnp.stack([res_state, zeros_field, res_adjoint, zeros_field])
        for bit_number in reversed(range(bit_count - 1)):
            packed = butterfly_segment(
                packed, bit_number, position, device, local_steps, horizon, False
            )
        right_side = jnp.stack([packed[:, 0] + packed[:, 1], packed[:, 0] - packed[:, 1]], 1)
        iterate = block_solve(right_side, shift_real, shift_imag, determinant)
        for sweep_index in range(1, SWEEPS):
            sweep_rimmed = extended(iterate, (("space", 2),), 1)
            pushed = right_side + step_size * neighbour_sum(sweep_rimmed, weights)
            iterate = block_solve(pushed, shift_real, shift_imag, determinant)
        packed = jnp.stack(
            [0.5 * (iterate[:, 0] + iterate[:, 1]), 0.5 * (iterate[:, 0] - iterate[:, 1])], 1
        )
        for bit_number in range(bit_count - 1):
            packed = butterfly_segment(
                packed, bit_number, position, device, local_steps, horizon, True
            )
        state_delta = packed[0]
        adjoint_delta = packed[2]
        state_now = state_now + state_delta
        adjoint_now = adjoint_now + adjoint_delta
    return (state_now, adjoint_now)


def solution(mesh):
    in_specs = (
        P("tm", "space", None, None),
        P("tm", "space", None, None),
        P("tm", "space", None, None),
        P("space", None, None),
        P("space", None, None),
    )
    out_specs = (P("tm", "space", None, None), P("tm", "space", None, None))
    return jax.shard_map(
        on_device, mesh=mesh, in_specs=in_specs, out_specs=out_specs, check_vma=False
    )
```

profile of v0, /device:TPU:16, one launch (start us, length us, event | category | flops | bytes accessed | tf_op | source)
XLA Modules:
  0.0 320.3 jit_solution(7775308368810553859)
XLA Ops:
  5.7 3.3 %collective-permute-start = (f32[1,96,128]{2,1,0:T(8,128)S(1)}, f32[1,96,128]{2,1,0:T(8,128)S(1)}, u32[]{:S(2)}, u32[]{:S(2)}) collective-permute-start(f32[1,96,128]{2,1,0:T(8,128)S(1)} %get-tuple-element.126), channel_id=1, source_target_pairs={{1,0},{2,1},{3,2},{4,3},{5,4},{6,5},{7,6},{9,8},{10,9},{11,10},{12... | collective-permute-start | bytes 147464 | tf_op jit(solution)/shard_map/ppermute | solution.py:36
  9.0 2.6 collective-permute-start.1
  12.8 4.2 %collective-permute-start.4 = (f32[2,4,1,96,128]{4,3,2,1,0:T(8,128)S(1)}, f32[2,4,1,96,128]{4,3,2,1,0:T(8,128)S(1)}, u32[]{:S(2)}, u32[]{:S(2)}) collective-permute-start(f32[2,4,1,96,128]{4,3,2,1,0:T(8,128)S(1)} %get-tuple-element.121), channel_id=1, source_target_pairs={{1,0},{2,1},{3,2},{4,3},{5,4},{6,5},{7,6},{9,8},{10,9},{11,10},{12... | collective-permute-start | bytes 1179656 | tf_op jit(solution)/shard_map/ppermute | solution.py:36
  19.4 14.9 %collective-permute-done.4 = f32[2,4,1,96,128]{4,3,2,1,0:T(8,128)S(1)} collective-permute-done((f32[2,4,1,96,128]{4,3,2,1,0:T(8,128)S(1)}, f32[2,4,1,96,128]{4,3,2,1,0:T(8,128)S(1)}, u32[]{:S(2)}, u32[]{:S(2)}) %collective-permute-start.4) | collective-permute-done | bytes 393248 | tf_op jit(solution)/shard_map/ppermute | solution.py:36
  38.5 18.3 %collective-permute-done.6 = f32[4,2,2,96,128]{4,3,2,1,0:T(8,128)S(1)} collective-permute-done((f32[4,2,2,96,128]{4,3,2,1,0:T(8,128)S(1)}, f32[4,2,2,96,128]{4,3,2,1,0:T(8,128)S(1)}, u32[]{:S(2)}, u32[]{:S(2)}) %collective-permute-start.6) | collective-permute-done | bytes 786464 | tf_op jit(solution)/shard_map/ppermute | solution.py:23
  58.3 2.5 collective-permute-done.7
  64.2 4.1 %collective-permute-start.8 = (f32[4,2,1,96,128]{4,3,2,1,0:T(8,128)S(1)}, f32[4,2,1,96,128]{4,3,2,1,0:T(8,128)S(1)}, u32[]{:S(2)}, u32[]{:S(2)}) collective-permute-start(f32[4,2,1,96,128]{4,3,2,1,0:T(8,128)S(1)} %get-tuple-element.117), channel_id=1, source_target_pairs={{1,0},{2,1},{3,2},{4,3},{5,4},{6,5},{7,6},{9,8},{10,9},{11,10},{12... | collective-permute-start | bytes 1179656 | tf_op jit(solution)/shard_map/ppermute | solution.py:36
  70.4 15.9 %collective-permute-done.8 = f32[4,2,1,96,128]{4,3,2,1,0:T(8,128)S(1)} collective-permute-done((f32[4,2,1,96,128]{4,3,2,1,0:T(8,128)S(1)}, f32[4,2,1,96,128]{4,3,2,1,0:T(8,128)S(1)}, u32[]{:S(2)}, u32[]{:S(2)}) %collective-permute-start.8) | collective-permute-done | bytes 393248 | tf_op jit(solution)/shard_map/ppermute | solution.py:36
  86.4 2.2 select_maximum_fusion.25
  89.8 4.3 %collective-permute-start.10 = (f32[4,2,1,96,128]{4,3,2,1,0:T(8,128)S(1)}, f32[4,2,1,96,128]{4,3,2,1,0:T(8,128)S(1)}, u32[]{:S(2)}, u32[]{:S(2)}) collective-permute-start(f32[4,2,1,96,128]{4,3,2,1,0:T(8,128)S(1)} %get-tuple-element.115), channel_id=1, source_target_pairs={{1,0},{2,1},{3,2},{4,3},{5,4},{6,5},{7,6},{9,8},{10,9},{11,10},{12... | collective-permute-start | bytes 1179656 | tf_op jit(solution)/shard_map/ppermute | solution.py:36
  96.1 15.8 %collective-permute-done.10 = f32[4,2,1,96,128]{4,3,2,1,0:T(8,128)S(1)} collective-permute-done((f32[4,2,1,96,128]{4,3,2,1,0:T(8,128)S(1)}, f32[4,2,1,96,128]{4,3,2,1,0:T(8,128)S(1)}, u32[]{:S(2)}, u32[]{:S(2)}) %collective-permute-start.10) | collective-permute-done | bytes 393248 | tf_op jit(solution)/shard_map/ppermute | solution.py:36
  112.1 2.2 select_maximum_fusion.20
  115.5 4.3 %collective-permute-start.12 = (f32[4,2,1,96,128]{4,3,2,1,0:T(8,128)S(1)}, f32[4,2,1,96,128]{4,3,2,1,0:T(8,128)S(1)}, u32[]{:S(2)}, u32[]{:S(2)}) collective-permute-start(f32[4,2,1,96,128]{4,3,2,1,0:T(8,128)S(1)} %get-tuple-element.113), channel_id=1, source_target_pairs={{1,0},{2,1},{3,2},{4,3},{5,4},{6,5},{7,6},{9,8},{10,9},{11,10},{12... | collective-permute-start | bytes 1179656 | tf_op jit(solution)/shard_map/ppermute | solution.py:36
  122.0 15.6 %collective-permute-done.12 = f32[4,2,1,96,128]{4,3,2,1,0:T(8,128)S(1)} collective-permute-done((f32[4,2,1,96,128]{4,3,2,1,0:T(8,128)S(1)}, f32[4,2,1,96,128]{4,3,2,1,0:T(8,128)S(1)}, u32[]{:S(2)}, u32[]{:S(2)}) %collective-permute-start.12) | collective-permute-done | bytes 393248 | tf_op jit(solution)/shard_map/ppermute | solution.py:36
  137.7 2.2 select_maximum_fusion.15
  145.5 18.2 %collective-permute-done.15 = f32[4,2,2,96,128]{4,3,2,1,0:T(8,128)S(1)} collective-permute-done((f32[4,2,2,96,128]{4,3,2,1,0:T(8,128)S(1)}, f32[4,2,2,96,128]{4,3,2,1,0:T(8,128)S(1)}, u32[]{:S(2)}, u32[]{:S(2)}) %collective-permute-start.15) | collective-permute-done | bytes 786464 | tf_op jit(solution)/shard_map/ppermute | solution.py:23
  167.3 3.5 %collective-permute-done.17 = f32[2,1,2,96,128]{4,3,2,1,0:T(8,128)S(1)} collective-permute-done((f32[2,1,2,96,128]{4,3,2,1,0:T(8,128)S(1)}, f32[2,1,2,96,128]{4,3,2,1,0:T(8,128)S(1)}, u32[]{:S(2)}, u32[]{:S(2)}) %collective-permute-start.17) | collective-permute-done | bytes 196640 | tf_op jit(solution)/shard_map/ppermute | solution.py:36
  171.0 4.3 %collective-permute-start.18 = (f32[2,4,1,96,128]{4,3,2,1,0:T(8,128)S(1)}, f32[2,4,1,96,128]{4,3,2,1,0:T(8,128)S(1)}, u32[]{:S(2)}, u32[]{:S(2)}) collective-permute-start(f32[2,4,1,96,128]{4,3,2,1,0:T(8,128)S(1)} %get-tuple-element.107), channel_id=1, source_target_pairs={{1,0},{2,1},{3,2},{4,3},{5,4},{6,5},{7,6},{9,8},{10,9},{11,10},{12... | collective-permute-start | bytes 1179656 | tf_op jit(solution)/shard_map/ppermute | solution.py:36
  177.4 12.8 %collective-permute-done.18 = f32[2,4,1,96,128]{4,3,2,1,0:T(8,128)S(1)} collective-permute-done((f32[2,4,1,96,128]{4,3,2,1,0:T(8,128)S(1)}, f32[2,4,1,96,128]{4,3,2,1,0:T(8,128)S(1)}, u32[]{:S(2)}, u32[]{:S(2)}) %collective-permute-start.18) | collective-permute-done | bytes 393248 | tf_op jit(solution)/shard_map/ppermute | solution.py:36
  190.3 3.8 %collective-permute-done.19 = f32[2,4,1,96,128]{4,3,2,1,0:T(8,128)S(1)} collective-permute-done((f32[2,4,1,96,128]{4,3,2,1,0:T(8,128)S(1)}, f32[2,4,1,96,128]{4,3,2,1,0:T(8,128)S(1)}, u32[]{:S(2)}, u32[]{:S(2)}) %collective-permute-start.19) | collective-permute-done | bytes 393248 | tf_op jit(solution)/shard_map/ppermute | solution.py:34
  195.4 19.7 %collective-permute-done.20 = f32[4,2,2,96,128]{4,3,2,1,0:T(8,128)S(1)} collective-permute-done((f32[4,2,2,96,128]{4,3,2,1,0:T(8,128)S(1)}, f32[4,2,2,96,128]{4,3,2,1,0:T(8,128)S(1)}, u32[]{:S(2)}, u32[]{:S(2)}) %collective-permute-start.20) | collective-permute-done | bytes 786464 | tf_op jit(solution)/shard_map/ppermute | solution.py:23
  215.6 2.3 collective-permute-done.21
  219.1 4.1 %collective-permute-start.22 = (f32[4,2,1,96,128]{4,3,2,1,0:T(8,128)S(1)}, f32[4,2,1,96,128]{4,3,2,1,0:T(8,128)S(1)}, u32[]{:S(2)}, u32[]{:S(2)}) collective-permute-start(f32[4,2,1,96,128]{4,3,2,1,0:T(8,128)S(1)} %get-tuple-element.103), channel_id=1, source_target_pairs={{1,0},{2,1},{3,2},{4,3},{5,4},{6,5},{7,6},{9,8},{10,9},{11,10},{12... | collective-permute-start | bytes 1179656 | tf_op jit(solution)/shard_map/ppermute | solution.py:36
  225.2 15.9 %collective-permute-done.22 = f32[4,2,1,96,128]{4,3,2,1,0:T(8,128)S(1)} collective-permute-done((f32[4,2,1,96,128]{4,3,2,1,0:T(8,128)S(1)}, f32[4,2,1,96,128]{4,3,2,1,0:T(8,128)S(1)}, u32[]{:S(2)}, u32[]{:S(2)}) %collective-permute-start.22) | collective-permute-done | bytes 393248 | tf_op jit(solution)/shard_map/ppermute | solution.py:36
  241.3 2.2 select_maximum_fusion.10
  244.7 4.3 %collective-permute-start.24 = (f32[4,2,1,96,128]{4,3,2,1,0:T(8,128)S(1)}, f32[4,2,1,96,128]{4,3,2,1,0:T(8,128)S(1)}, u32[]{:S(2)}, u32[]{:S(2)}) collective-permute-start(f32[4,2,1,96,128]{4,3,2,1,0:T(8,128)S(1)} %get-tuple-element.101), channel_id=1, source_target_pairs={{1,0},{2,1},{3,2},{4,3},{5,4},{6,5},{7,6},{9,8},{10,9},{11,10},{12... | collective-permute-start | bytes 1179656 | tf_op jit(solution)/shard_map/ppermute | solution.py:36
  249.0 2.3 collective-permute-start.25
  251.2 15.6 %collective-permute-done.24 = f32[4,2,1,96,128]{4,3,2,1,0:T(8,128)S(1)} collective-permute-done((f32[4,2,1,96,128]{4,3,2,1,0:T(8,128)S(1)}, f32[4,2,1,96,128]{4,3,2,1,0:T(8,128)S(1)}, u32[]{:S(2)}, u32[]{:S(2)}) %collective-permute-start.24) | collective-permute-done | bytes 393248 | tf_op jit(solution)/shard_map/ppermute | solution.py:36
  270.4 4.3 %collective-permute-start.26 = (f32[4,2,1,96,128]{4,3,2,1,0:T(8,128)S(1)}, f32[4,2,1,96,128]{4,3,2,1,0:T(8,128)S(1)}, u32[]{:S(2)}, u32[]{:S(2)}) collective-permute-start(f32[4,2,1,96,128]{4,3,2,1,0:T(8,128)S(1)} %get-tuple-element.99), channel_id=1, source_target_pairs={{1,0},{2,1},{3,2},{4,3},{5,4},{6,5},{7,6},{9,8},{10,9},{11,10},{12... | collective-permute-start | bytes 1179656 | tf_op jit(solution)/shard_map/ppermute | solution.py:36
  276.7 15.8 %collective-permute-done.26 = f32[4,2,1,96,128]{4,3,2,1,0:T(8,128)S(1)} collective-permute-done((f32[4,2,1,96,128]{4,3,2,1,0:T(8,128)S(1)}, f32[4,2,1,96,128]{4,3,2,1,0:T(8,128)S(1)}, u32[]{:S(2)}, u32[]{:S(2)}) %collective-permute-start.26) | collective-permute-done | bytes 393248 | tf_op jit(solution)/shard_map/ppermute | solution.py:36
  296.2 2.3 collective-permute-done.28
  299.4 19.3 %collective-permute-done.29 = f32[4,2,2,96,128]{4,3,2,1,0:T(8,128)S(1)} collective-permute-done((f32[4,2,2,96,128]{4,3,2,1,0:T(8,128)S(1)}, f32[4,2,2,96,128]{4,3,2,1,0:T(8,128)S(1)}, u32[]{:S(2)}, u32[]{:S(2)}) %collective-permute-start.29) | collective-permute-done | bytes 786464 | tf_op jit(solution)/shard_map/ppermute | solution.py:23
  (127 shorter events, 56.0 us)
Async XLA Ops:
  0.6 35.2 %copy-start.1 = (f32[2,2,96,128]{3,2,1,0:T(8,128)S(1)}, f32[2,2,96,128]{3,2,1,0:T(8,128)}, u32[]{:S(2)}) copy-start(f32[2,2,96,128]{3,2,1,0:T(8,128)} %param.5) | copy-start | bytes 589828
  0.6 35.1 %copy-start = (f32[2,2,96,128]{3,2,1,0:T(8,128)S(1)}, f32[2,2,96,128]{3,2,1,0:T(8,128)}, u32[]{:S(2)}) copy-start(f32[2,2,96,128]{3,2,1,0:T(8,128)} %param.6) | copy-start | bytes 589828
  1.8 9.7 %collective-permute-start.2 = (f32[2,1,2,96,128]{4,3,2,1,0:T(8,128)S(1)}, f32[2,1,2,96,128]{4,3,2,1,0:T(8,128)S(1)}, u32[]{:S(2)}, u32[]{:S(2)}) collective-permute-start(f32[2,1,2,96,128]{4,3,2,1,0:T(8,128)S(1)} %get-tuple-element.124), channel_id=1, source_target_pairs={{0,8},{8,16},{16,24},{1,9},{9,17},{17,25},{2,10},{10,18},{18,26},{... | collective-permute-start | bytes 589832 | tf_op jit(solution)/shard_map/ppermute | solution.py:34
  3.6 8.0 %collective-permute-start.3 = (f32[2,1,2,96,128]{4,3,2,1,0:T(8,128)S(1)}, f32[2,1,2,96,128]{4,3,2,1,0:T(8,128)S(1)}, u32[]{:S(2)}, u32[]{:S(2)}) collective-permute-start(f32[2,1,2,96,128]{4,3,2,1,0:T(8,128)S(1)} %get-tuple-element.125), channel_id=1, source_target_pairs={{8,0},{16,8},{24,16},{9,1},{17,9},{25,17},{10,2},{18,10},{26,18},{... | collective-permute-start | bytes 589832 | tf_op jit(solution)/shard_map/ppermute | solution.py:36
  5.7 13.3 %collective-permute-start = (f32[1,96,128]{2,1,0:T(8,128)S(1)}, f32[1,96,128]{2,1,0:T(8,128)S(1)}, u32[]{:S(2)}, u32[]{:S(2)}) collective-permute-start(f32[1,96,128]{2,1,0:T(8,128)S(1)} %get-tuple-element.126), channel_id=1, source_target_pairs={{1,0},{2,1},{3,2},{4,3},{5,4},{6,5},{7,6},{9,8},{10,9},{11,10},{12... | collective-permute-start | bytes 147464 | tf_op jit(solution)/shard_map/ppermute | solution.py:36
  9.0 10.0 %collective-permute-start.1 = (f32[1,96,128]{2,1,0:T(8,128)S(1)}, f32[1,96,128]{2,1,0:T(8,128)S(1)}, u32[]{:S(2)}, u32[]{:S(2)}) collective-permute-start(f32[1,96,128]{2,1,0:T(8,128)S(1)} %get-tuple-element.127), channel_id=1, source_target_pairs={{0,1},{1,2},{2,3},{3,4},{4,5},{5,6},{6,7},{8,9},{9,10},{10,11},{11... | collective-permute-start | bytes 147464 | tf_op jit(solution)/shard_map/ppermute | solution.py:34
  12.8 21.5 %collective-permute-start.4 = (f32[2,4,1,96,128]{4,3,2,1,0:T(8,128)S(1)}, f32[2,4,1,96,128]{4,3,2,1,0:T(8,128)S(1)}, u32[]{:S(2)}, u32[]{:S(2)}) collective-permute-start(f32[2,4,1,96,128]{4,3,2,1,0:T(8,128)S(1)} %get-tuple-element.121), channel_id=1, source_target_pairs={{1,0},{2,1},{3,2},{4,3},{5,4},{6,5},{7,6},{9,8},{10,9},{11,10},{12... | collective-permute-start | bytes 1179656 | tf_op jit(solution)/shard_map/ppermute | solution.py:36
  16.9 18.8 %collective-permute-start.5 = (f32[2,4,1,96,128]{4,3,2,1,0:T(8,128)S(1)}, f32[2,4,1,96,128]{4,3,2,1,0:T(8,128)S(1)}, u32[]{:S(2)}, u32[]{:S(2)}) collective-permute-start(f32[2,4,1,96,128]{4,3,2,1,0:T(8,128)S(1)} %get-tuple-element.120), channel_id=1, source_target_pairs={{0,1},{1,2},{2,3},{3,4},{4,5},{5,6},{6,7},{8,9},{9,10},{10,11},{11... | collective-permute-start | bytes 1179656 | tf_op jit(solution)/shard_map/ppermute | solution.py:34
  37.0 19.8 %collective-permute-start.6 = (f32[4,2,2,96,128]{4,3,2,1,0:T(8,128)S(1)}, f32[4,2,2,96,128]{4,3,2,1,0:T(8,128)S(1)}, u32[]{:S(2)}, u32[]{:S(2)}) collective-permute-start(f32[4,2,2,96,128]{4,3,2,1,0:T(8,128)S(1)} %pad_maximum_fusion.5), channel_id=1, source_target_pairs={{0,16},{16,0},{8,24},{24,8},{1,17},{17,1},{9,25},{25,9},{2,18},{18... | collective-permute-start | bytes 2359304 | tf_op jit(solution)/shard_map/ppermute | solution.py:23
  58.1 2.6 collective-permute-start.7
  64.2 22.1 %collective-permute-start.8 = (f32[4,2,1,96,128]{4,3,2,1,0:T(8,128)S(1)}, f32[4,2,1,96,128]{4,3,2,1,0:T(8,128)S(1)}, u32[]{:S(2)}, u32[]{:S(2)}) collective-permute-start(f32[4,2,1,96,128]{4,3,2,1,0:T(8,128)S(1)} %get-tuple-element.117), channel_id=1, source_target_pairs={{1,0},{2,1},{3,2},{4,3},{5,4},{6,5},{7,6},{9,8},{10,9},{11,10},{12... | collective-permute-start | bytes 1179656 | tf_op jit(solution)/shard_map/ppermute | solution.py:36
  68.3 18.1 %collective-permute-start.9 = (f32[4,2,1,96,128]{4,3,2,1,0:T(8,128)S(1)}, f32[4,2,1,96,128]{4,3,2,1,0:T(8,128)S(1)}, u32[]{:S(2)}, u32[]{:S(2)}) collective-permute-start(f32[4,2,1,96,128]{4,3,2,1,0:T(8,128)S(1)} %get-tuple-element.116), channel_id=1, source_target_pairs={{0,1},{1,2},{2,3},{3,4},{4,5},{5,6},{6,7},{8,9},{9,10},{10,11},{11... | collective-permute-start | bytes 1179656 | tf_op jit(solution)/shard_map/ppermute | solution.py:34
  89.8 22.1 %collective-permute-start.10 = (f32[4,2,1,96,128]{4,3,2,1,0:T(8,128)S(1)}, f32[4,2,1,96,128]{4,3,2,1,0:T(8,128)S(1)}, u32[]{:S(2)}, u32[]{:S(2)}) collective-permute-start(f32[4,2,1,96,128]{4,3,2,1,0:T(8,128)S(1)} %get-tuple-element.115), channel_id=1, source_target_pairs={{1,0},{2,1},{3,2},{4,3},{5,4},{6,5},{7,6},{9,8},{10,9},{11,10},{12... | collective-permute-start | bytes 1179656 | tf_op jit(solution)/shard_map/ppermute | solution.py:36
  94.1 18.0 %collective-permute-start.11 = (f32[4,2,1,96,128]{4,3,2,1,0:T(8,128)S(1)}, f32[4,2,1,96,128]{4,3,2,1,0:T(8,128)S(1)}, u32[]{:S(2)}, u32[]{:S(2)}) collective-permute-start(f32[4,2,1,96,128]{4,3,2,1,0:T(8,128)S(1)} %get-tuple-element.114), channel_id=1, source_target_pairs={{0,1},{1,2},{2,3},{3,4},{4,5},{5,6},{6,7},{8,9},{9,10},{10,11},{11... | collective-permute-start | bytes 1179656 | tf_op jit(solution)/shard_map/ppermute | solution.py:34
  115.5 22.1 %collective-permute-start.12 = (f32[4,2,1,96,128]{4,3,2,1,0:T(8,128)S(1)}, f32[4,2,1,96,128]{4,3,2,1,0:T(8,128)S(1)}, u32[]{:S(2)}, u32[]{:S(2)}) collective-permute-start(f32[4,2,1,96,128]{4,3,2,1,0:T(8,128)S(1)} %get-tuple-element.113), channel_id=1, source_target_pairs={{1,0},{2,1},{3,2},{4,3},{5,4},{6,5},{7,6},{9,8},{10,9},{11,10},{12... | collective-permute-start | bytes 1179656 | tf_op jit(solution)/shard_map/ppermute | solution.py:36
  119.8 18.0 %collective-permute-start.13 = (f32[4,2,1,96,128]{4,3,2,1,0:T(8,128)S(1)}, f32[4,2,1,96,128]{4,3,2,1,0:T(8,128)S(1)}, u32[]{:S(2)}, u32[]{:S(2)}) collective-permute-start(f32[4,2,1,96,128]{4,3,2,1,0:T(8,128)S(1)} %get-tuple-element.112), channel_id=1, source_target_pairs={{0,1},{1,2},{2,3},{3,4},{4,5},{5,6},{6,7},{8,9},{9,10},{10,11},{11... | collective-permute-start | bytes 1179656 | tf_op jit(solution)/shard_map/ppermute | solution.py:34
  141.2 2.4 collective-permute-start.14
  144.1 19.6 %collective-permute-start.15 = (f32[4,2,2,96,128]{4,3,2,1,0:T(8,128)S(1)}, f32[4,2,2,96,128]{4,3,2,1,0:T(8,128)S(1)}, u32[]{:S(2)}, u32[]{:S(2)}) collective-permute-start(f32[4,2,2,96,128]{4,3,2,1,0:T(8,128)S(1)} %fusion.63), channel_id=1, source_target_pairs={{0,16},{16,0},{8,24},{24,8},{1,17},{17,1},{9,25},{25,9},{2,18},{18... | collective-permute-start | bytes 2359304 | tf_op jit(solution)/shard_map/ppermute | solution.py:23
  164.7 2.6 collective-permute-start.16
  166.0 4.8 %collective-permute-start.17 = (f32[2,1,2,96,128]{4,3,2,1,0:T(8,128)S(1)}, f32[2,1,2,96,128]{4,3,2,1,0:T(8,128)S(1)}, u32[]{:S(2)}, u32[]{:S(2)}) collective-permute-start(f32[2,1,2,96,128]{4,3,2,1,0:T(8,128)S(1)} %get-tuple-element.123), channel_id=1, source_target_pairs={{8,0},{16,8},{24,16},{9,1},{17,9},{25,17},{10,2},{18,10},{26,18},{... | collective-permute-start | bytes 589832 | tf_op jit(solution)/shard_map/ppermute | solution.py:36
  171.0 19.3 %collective-permute-start.18 = (f32[2,4,1,96,128]{4,3,2,1,0:T(8,128)S(1)}, f32[2,4,1,96,128]{4,3,2,1,0:T(8,128)S(1)}, u32[]{:S(2)}, u32[]{:S(2)}) collective-permute-start(f32[2,4,1,96,128]{4,3,2,1,0:T(8,128)S(1)} %get-tuple-element.107), channel_id=1, source_target_pairs={{1,0},{2,1},{3,2},{4,3},{5,4},{6,5},{7,6},{9,8},{10,9},{11,10},{12... | collective-permute-start | bytes 1179656 | tf_op jit(solution)/shard_map/ppermute | solution.py:36
  175.3 18.8 %collective-permute-start.19 = (f32[2,4,1,96,128]{4,3,2,1,0:T(8,128)S(1)}, f32[2,4,1,96,128]{4,3,2,1,0:T(8,128)S(1)}, u32[]{:S(2)}, u32[]{:S(2)}) collective-permute-start(f32[2,4,1,96,128]{4,3,2,1,0:T(8,128)S(1)} %get-tuple-element.106), channel_id=1, source_target_pairs={{0,1},{1,2},{2,3},{3,4},{4,5},{5,6},{6,7},{8,9},{9,10},{10,11},{11... | collective-permute-start | bytes 1179656 | tf_op jit(solution)/shard_map/ppermute | solution.py:34
  195.3 19.8 %collective-permute-start.20 = (f32[4,2,2,96,128]{4,3,2,1,0:T(8,128)S(1)}, f32[4,2,2,96,128]{4,3,2,1,0:T(8,128)S(1)}, u32[]{:S(2)}, u32[]{:S(2)}) collective-permute-start(f32[4,2,2,96,128]{4,3,2,1,0:T(8,128)S(1)} %pad_maximum_fusion.4), channel_id=1, source_target_pairs={{0,16},{16,0},{8,24},{24,8},{1,17},{17,1},{9,25},{25,9},{2,18},{18... | collective-permute-start | bytes 2359304 | tf_op jit(solution)/shard_map/ppermute | solution.py:23
  215.5 2.4 collective-permute-start.21
  219.1 22.0 %collective-permute-start.22 = (f32[4,2,1,96,128]{4,3,2,1,0:T(8,128)S(1)}, f32[4,2,1,96,128]{4,3,2,1,0:T(8,128)S(1)}, u32[]{:S(2)}, u32[]{:S(2)}) collective-permute-start(f32[4,2,1,96,128]{4,3,2,1,0:T(8,128)S(1)} %get-tuple-element.103), channel_id=1, source_target_pairs={{1,0},{2,1},{3,2},{4,3},{5,4},{6,5},{7,6},{9,8},{10,9},{11,10},{12... | collective-permute-start | bytes 1179656 | tf_op jit(solution)/shard_map/ppermute | solution.py:36
  223.2 18.1 %collective-permute-start.23 = (f32[4,2,1,96,128]{4,3,2,1,0:T(8,128)S(1)}, f32[4,2,1,96,128]{4,3,2,1,0:T(8,128)S(1)}, u32[]{:S(2)}, u32[]{:S(2)}) collective-permute-start(f32[4,2,1,96,128]{4,3,2,1,0:T(8,128)S(1)} %get-tuple-element.102), channel_id=1, source_target_pairs={{0,1},{1,2},{2,3},{3,4},{4,5},{5,6},{6,7},{8,9},{9,10},{10,11},{11... | collective-permute-start | bytes 1179656 | tf_op jit(solution)/shard_map/ppermute | solution.py:34
  244.7 22.1 %collective-permute-start.24 = (f32[4,2,1,96,128]{4,3,2,1,0:T(8,128)S(1)}, f32[4,2,1,96,128]{4,3,2,1,0:T(8,128)S(1)}, u32[]{:S(2)}, u32[]{:S(2)}) collective-permute-start(f32[4,2,1,96,128]{4,3,2,1,0:T(8,128)S(1)} %get-tuple-element.101), channel_id=1, source_target_pairs={{1,0},{2,1},{3,2},{4,3},{5,4},{6,5},{7,6},{9,8},{10,9},{11,10},{12... | collective-permute-start | bytes 1179656 | tf_op jit(solution)/shard_map/ppermute | solution.py:36
  249.0 18.0 %collective-permute-start.25 = (f32[4,2,1,96,128]{4,3,2,1,0:T(8,128)S(1)}, f32[4,2,1,96,128]{4,3,2,1,0:T(8,128)S(1)}, u32[]{:S(2)}, u32[]{:S(2)}) collective-permute-start(f32[4,2,1,96,128]{4,3,2,1,0:T(8,128)S(1)} %get-tuple-element.100), channel_id=1, source_target_pairs={{0,1},{1,2},{2,3},{3,4},{4,5},{5,6},{6,7},{8,9},{9,10},{10,11},{11... | collective-permute-start | bytes 1179656 | tf_op jit(solution)/shard_map/ppermute | solution.py:34
  270.4 22.1 %collective-permute-start.26 = (f32[4,2,1,96,128]{4,3,2,1,0:T(8,128)S(1)}, f32[4,2,1,96,128]{4,3,2,1,0:T(8,128)S(1)}, u32[]{:S(2)}, u32[]{:S(2)}) collective-permute-start(f32[4,2,1,96,128]{4,3,2,1,0:T(8,128)S(1)} %get-tuple-element.99), channel_id=1, source_target_pairs={{1,0},{2,1},{3,2},{4,3},{5,4},{6,5},{7,6},{9,8},{10,9},{11,10},{12... | collective-permute-start | bytes 1179656 | tf_op jit(solution)/shard_map/ppermute | solution.py:36
  274.6 18.0 %collective-permute-start.27 = (f32[4,2,1,96,128]{4,3,2,1,0:T(8,128)S(1)}, f32[4,2,1,96,128]{4,3,2,1,0:T(8,128)S(1)}, u32[]{:S(2)}, u32[]{:S(2)}) collective-permute-start(f32[4,2,1,96,128]{4,3,2,1,0:T(8,128)S(1)} %get-tuple-element.98), channel_id=1, source_target_pairs={{0,1},{1,2},{2,3},{3,4},{4,5},{5,6},{6,7},{8,9},{9,10},{10,11},{11... | collective-permute-start | bytes 1179656 | tf_op jit(solution)/shard_map/ppermute | solution.py:34
  296.1 2.4 collective-permute-start.28
  299.0 19.6 %collective-permute-start.29 = (f32[4,2,2,96,128]{4,3,2,1,0:T(8,128)S(1)}, f32[4,2,2,96,128]{4,3,2,1,0:T(8,128)S(1)}, u32[]{:S(2)}, u32[]{:S(2)}) collective-permute-start(f32[4,2,2,96,128]{4,3,2,1,0:T(8,128)S(1)} %fusion.69), channel_id=1, source_target_pairs={{0,16},{16,0},{8,24},{24,8},{1,17},{17,1},{9,25},{25,9},{2,18},{18... | collective-permute-start | bytes 2359304 | tf_op jit(solution)/shard_map/ppermute | solution.py:23
  (4 other events, 73.8 us)
where the time goes:
time: 323 us; the launch traced here: 320 us
  waiting for transfers between devices  217 us (67%)
  starting transfers between devices  65.5 us (20%)
  other arithmetic  35.2 us (11%)
    ppermute x11, waiting for transfers between devices, extended(): lax.ppermute(head, axis, [((i + 1) % count, i) for i in range(ends)])  126 us
    ppermute x8, waiting for transfers between devices, swapped(): return lax.ppermute(block, axis, route)  84.8 us
    ppermute x11, starting transfers between devices, extended(): lax.ppermute(head, axis, [((i + 1) % count, i) for i in range(ends)])  39.6 us
    ppermute x11, starting transfers between devices, extended(): lax.ppermute(tail, axis, [(i, (i + 1) % count) for i in range(ends)])  22.4 us
    concatenate x11, other arithmetic, extended(): jnp.concatenate([lax.ppermute(tail, axis, [(i, (i + 1) % count) for i in...  15.7 us
  transfers between devices with their start and end apart: 30, of which 25 were waited for; matrix products, arithmetic and copies ran while one was open for 1% of the time, Pallas kernels for 0%

commit v1 on v0

v1 whole, which is shorter than its diff:
```python
import math

import jax
import jax.numpy as jnp
from jax import lax
from jax.experimental import pallas as pl
from jax.experimental.pallas import tpu as pltpu
from jax.sharding import PartitionSpec as P

SWEEPS = 4
OUTER = 2

TAU = 0.25
GAMMA = 0.05
MESH = pl.DeviceIdType.MESH

POOL = 2
PARTS = 4


def turn(pair, angle):
    re, im = pair
    c, s = math.cos(angle), math.sin(angle)
    if im is None:
        return re * c, re * -s
    return re * c + im * s, im * c - re * s


def rfft(xs):
    n = len(xs)
    if n == 1:
        return [(xs[0], None)]
    if n == 2:
        return [(xs[0] + xs[1], None), (xs[0] - xs[1], None)]
    even, odd = rfft(xs[::2]), rfft(xs[1::2])
    out = [None] * (n // 2 + 1)
    out[0] = (even[0][0] + odd[0][0], None)
    out[n // 2] = (even[0][0] - odd[0][0], None)
    out[n // 4] = (even[n // 4][0], -odd[n // 4][0])
    for k in range(1, n // 4):
        er, ei = even[k]
        pr, pi = turn(odd[k], 2.0 * math.pi * k / n)
        out[k] = (er + pr, ei + pi)
        out[n // 2 - k] = (er - pr, pi - ei)
    return out


def irfft(modes):
    n = 2 * (len(modes) - 1)
    if n == 2:
        return [modes[0][0] + modes[1][0], modes[0][0] - modes[1][0]]
    even = [None] * (n // 4 + 1)
    odd = [None] * (n // 4 + 1)
    even[0] = (modes[0][0] + modes[n // 2][0], None)
    odd[0] = (modes[0][0] - modes[n // 2][0], None)
    even[n // 4] = (2.0 * modes[n // 4][0], None)
    odd[n // 4] = (-2.0 * modes[n // 4][1], None)
    for k in range(1, n // 4):
        ar, ai = modes[k]
        br, bi = modes[n // 2 - k]
        even[k] = (ar + br, ai - bi)
        odd[k] = turn((ar - br, ai + bi), -2.0 * math.pi * k / n)
    evens, odds = irfft(even), irfft(odd)
    out = []
    for a, b in zip(evens, odds):
        out += [a, b]
    return out


def make_kernel(T, S, LS, LP, NY, NZ):
    H = T * LS
    G = H // 2
    PX = POOL * T // PARTS
    PXS = PX // POOL
    PL = POOL * LP // PX
    R = NY // PARTS
    W = min(R + 16, NY)
    NXB = (S // POOL) * PX
    f32 = jnp.float32

    def q_of(th, si):
        return 2 * th + lax.rem(si + th, 2)

    def kernel(
        state_in, adjoint_in, target_in, initial_in, kappa_in, state_out, adjoint_out,
        raw, cur, hx, ey, hy, kap, ini, wt, dt, inv, that, fs, a0,
        a2a_send, a2a_recv, one_send, one_recv, ksend, krecv, hsend, hrecv, osend, orecv,
    ):
        t = lax.axis_index("tm")
        s = lax.axis_index("space")
        th, tl = t // PX, lax.rem(t, PX)
        so, si = s // POOL, lax.rem(s, POOL)
        q = q_of(th, si)
        x_at = so * PX + tl
        has = [x_at > 0, x_at < NXB - 1, q > 0, q < PARTS - 1]

        def place_q(qq):
            row = qq // 2
            return row, lax.rem(qq + row, 2)

        def beside(d):
            if d < 2:
                xx = x_at + (1 if d else -1)
                return {"tm": th * PX + lax.rem(xx, PX), "space": (xx // PX) * POOL + si}
            qq = q + (1 if d == 3 else -1)
            row, col = place_q(qq)
            return {"tm": row * PX + tl, "space": so * POOL + col}

        kap[...] = jnp.zeros_like(kap)
        hx[...] = jnp.zeros_like(hx)
        hy[...] = jnp.zeros_like(hy)
        barrier = pltpu.get_barrier_semaphore()
        members = POOL * T
        mine = si * T + t
        for off in range(1, members):
            other = lax.rem(mine + off, members)
            pl.semaphore_signal(
                barrier, inc=1,
                device_id={"tm": lax.rem(other, T), "space": so * POOL + other // T},
                device_id_type=MESH,
            )
        far_left = jnp.logical_and(tl == 0, so > 0)
        far_right = jnp.logical_and(tl == PX - 1, so < S // POOL - 1)
        for d, far in ((0, far_left), (1, far_right)):
            @pl.when(far)
            def _(d=d):
                pl.semaphore_signal(barrier, inc=1, device_id=beside(d), device_id_type=MESH)
        pl.semaphore_wait(
            barrier, members - 1 + jnp.where(far_left, 1, 0) + jnp.where(far_right, 1, 0)
        )

        def send(src, dst, ssem, rsem, tt, ss, wait=False):
            here = jnp.logical_and(tt == t, ss == s)

            @pl.when(here)
            def _():
                if not wait:
                    pltpu.make_async_copy(src, dst, rsem).start()

            @pl.when(jnp.logical_not(here))
            def _():
                copy = pltpu.make_async_remote_copy(
                    src_ref=src, dst_ref=dst, send_sem=ssem, recv_sem=rsem,
                    device_id={"tm": tt, "space": ss}, device_id_type=MESH,
                )
                if wait:
                    copy.wait_send()
                else:
                    copy.start()

        def arrived(dst, rsem):
            pltpu.make_async_copy(dst, dst, rsem).wait()

        def single(wait):
            col = lax.rem(tl, POOL)
            qd = q_of(th, col)
            tt = th * PX + si * PXS + tl // POOL
            ss = so * POOL + col
            planes = pl.ds((tl // POOL) * PL, PL)
            top = pl.multiple_of(jnp.clip(qd * R - 8, 0, NY - W), 8)
            low = pl.multiple_of(top - qd * R + 16, 8)
            send(
                kappa_in.at[planes, pl.ds(top, W)], kap.at[pl.ds(1, PL), pl.ds(low, W)],
                one_send.at[0], one_recv.at[0], tt, ss, wait,
            )
            send(
                initial_in.at[planes, pl.ds(pl.multiple_of(qd * R, 8), R)], ini,
                one_send.at[1], one_recv.at[1], tt, ss, wait,
            )

        def spread(wait):
            for a, source in enumerate((state_in, adjoint_in, target_in)):
                for off in (2, 1, 3, 0):
                    qd = lax.rem(q + off, PARTS)
                    row, col = place_q(qd)
                    for j in range(PXS):
                        tt = row * PX + si * PXS + j
                        send(
                            source.at[:, pl.ds(j * PL, PL), pl.ds(pl.multiple_of(qd * R, 8), R)],
                            raw.at[a, pl.ds(t * LS, LS)],
                            a2a_send.at[a, off, j], a2a_recv.at[a, t], tt, so * POOL + col, wait,
                        )

        single(False)
        spread(False)

        arrived(kap.at[pl.ds(1, PL), pl.ds(0, W)], one_recv.at[0])

        def kappa_copy(d):
            return pltpu.make_async_remote_copy(
                src_ref=kap.at[PL if d else 1, pl.ds(16, R)],
                dst_ref=kap.at[0 if d else PL + 1, pl.ds(16, R)],
                send_sem=ksend.at[d], recv_sem=krecv.at[1 - d],
                device_id=beside(d), device_id_type=MESH,
            )

        for d in (0, 1):
            @pl.when(has[d])
            def _(d=d):
                kappa_copy(d).start()
        for d in (0, 1):
            @pl.when(has[d])
            def _(d=d):
                edge = kap.at[PL + 1 if d else 0, pl.ds(16, R)]
                arrived(edge, krecv.at[d])
                kappa_copy(d).wait_send()

        lane = lax.broadcasted_iota(jnp.int32, (R, NZ), 1)
        for p in range(PL):
            here = kap[p + 1, 16 : 16 + R]
            tall = kap[p + 1, 8 : 24 + R]
            sides = [
                kap[p + 2, 16 : 16 + R],
                kap[p, 16 : 16 + R],
                pltpu.roll(tall, R + 15, 0)[8 : 8 + R],
                pltpu.roll(tall, 1, 0)[8 : 8 + R],
                jnp.where(lane == NZ - 1, 0.0, pltpu.roll(here, NZ - 1, 1)),
                jnp.where(lane == 0, 0.0, pltpu.roll(here, 1, 1)),
            ]
            faces = [0.5 * (here + beside_one) for beside_one in sides]
            total = faces[0]
            for face in faces[1:]:
                total = total + face
            faces[4] = jnp.where(lane == NZ - 1, 0.0, faces[4])
            faces[5] = jnp.where(lane == 0, 0.0, faces[5])
            for i, face in enumerate(faces):
                wt[i, p] = TAU * face
            dt[p] = TAU * total
            for k in range(G + 1):
                angle = 2.0 * math.pi * k / H
                b = math.sin(angle) if 0 < k < G else 0.0
                a = (1.0 - math.cos(angle)) + dt[p]
                inv[k, p] = 1.0 / (a * a + (b * b + TAU * TAU / GAMMA))

        def gather(a):
            for source in range(T):
                arrived(raw.at[a, pl.ds(source * LS, LS)], a2a_recv.at[a, source])

        def paired(modes):
            pairs = [(modes[0][0], modes[G][0])]
            for k in range(1, G):
                pairs.append(modes[k])
            return pairs

        def rows_out(par, g, v, p, value):
            ey[par, 0, g, v * PL + p : v * PL + p + 1] = value[0:1]
            ey[par, 1, g, v * PL + p : v * PL + p + 1] = value[R - 1 : R]

        def halo_copy(par, d, g):
            if d < 2:
                src = cur.at[par, g, :, PL - 1 if d else 0]
                dst = hx.at[par, 1 - d, g]
            else:
                src = ey.at[par, d - 2, g]
                dst = hy.at[par, 3 - d, g]
            return pltpu.make_async_remote_copy(
                src_ref=src, dst_ref=dst,
                send_sem=hsend.at[par, d, g], recv_sem=hrecv.at[par, d ^ 1, g],
                device_id=beside(d), device_id_type=MESH,
            )

        def halo_start(par, g, dirs=(0, 1, 2, 3)):
            for d in dirs:
                @pl.when(has[d])
                def _(d=d):
                    halo_copy(par, d, g).start()

        def halo_wait(par, g):
            for d in range(4):
                @pl.when(has[d])
                def _(d=d):
                    dst = hx.at[par, d, g] if d < 2 else hy.at[par, d - 2, g]
                    arrived(dst, hrecv.at[par, d, g])
                    halo_copy(par, d, g).wait_send()

        for a in range(2):
            gather(a)
            for p in range(PL):
                pairs = paired(rfft([raw[a, n, p] for n in range(H)]))
                for g, pair in enumerate(pairs):
                    for i in range(2):
                        cur[0, g, 2 * a + i, p] = pair[i]
                        rows_out(0, g, 2 * a + i, p, pair[i])
        for g in range(G):
            halo_start(0, g)
        arrived(ini, one_recv.at[1])
        for p in range(PL):
            fs[p] = ini[p] - raw[0, H - 1, p]
            a0[p] = raw[1, 0, p]
        gather(2)
        for p in range(PL):
            pairs = paired(rfft([raw[2, n, p] for n in range(H)]))
            for g, pair in enumerate(pairs):
                for i in range(2):
                    that[g, i, p] = -TAU * pair[i]
        single(True)
        spread(True)

        row_at = lax.broadcasted_iota(jnp.int32, (R, NZ), 0)
        coupling = TAU / GAMMA

        def spread_sum(par, g, v, p, weights):
            c = cur[par, g, v, p]
            left = hx[par, 0, g, v] if p == 0 else cur[par, g, v, p - 1]
            right = hx[par, 1, g, v] if p == PL - 1 else cur[par, g, v, p + 1]
            at = v * PL + p
            above = jnp.where(row_at == 0, hy[par, 0, g, at : at + 1], pltpu.roll(c, 1, 0))
            below = jnp.where(row_at == R - 1, hy[par, 1, g, at : at + 1], pltpu.roll(c, R - 1, 0))
            out = weights[0] * right + weights[1] * left
            out = out + (weights[2] * below + weights[3] * above)
            return out + (
                weights[4] * pltpu.roll(c, NZ - 1, 1) + weights[5] * pltpu.roll(c, 1, 1)
            )

        def sweep(par, g):
            nxt = 1 - par
            for p in range(PL):
                weights = [wt[i, p] for i in range(6)]
                ua, ub, pa, pb = [spread_sum(par, g, v, p, weights) for v in range(4)]
                ua = ua + fs[p]
                if g == 0:
                    ub = ub + fs[p]
                    pa = pa + (that[g, 0, p] - a0[p])
                    pb = pb + (that[g, 1, p] + a0[p])
                    low, high = dt[p], 2.0 + dt[p]
                    new = [
                        (low * ua - coupling * pa) * inv[0, p],
                        (high * ub - coupling * pb) * inv[G, p],
                        (TAU * ua + low * pa) * inv[0, p],
                        (TAU * ub + high * pb) * inv[G, p],
                    ]
                else:
                    c, b = math.cos(2.0 * math.pi * g / H), math.sin(2.0 * math.pi * g / H)
                    pa = pa + (that[g, 0, p] - c * a0[p])
                    pb = pb + (that[g, 1, p] - b * a0[p])
                    a = (1.0 - c) + dt[p]
                    scale = inv[g, p]
                    new = [
                        (a * ua + b * ub - coupling * pa) * scale,
                        (a * ub - b * ua - coupling * pb) * scale,
                        (TAU * ua + a * pa - b * pb) * scale,
                        (TAU * ub + a * pb + b * pa) * scale,
                    ]
                for v in range(4):
                    cur[nxt, g, v, p] = new[v]
                    rows_out(nxt, g, v, p, new[v])

        for outer in range(OUTER):
            start = outer * SWEEPS
            if outer:
                par = start % 2
                for p in range(PL):
                    last = cur[par, 0, 0, p] - cur[par, 0, 1, p]
                    first = cur[par, 0, 2, p] + cur[par, 0, 3, p]
                    for g in range(1, G):
                        angle = 2.0 * math.pi * g / H
                        last = last + (2.0 * math.cos(angle)) * cur[par, g, 0, p]
                        last = last + (2.0 * math.sin(angle)) * cur[par, g, 1, p]
                        first = first + 2.0 * cur[par, g, 2, p]
                    fs[p] = ini[p] - last * (1.0 / H)
                    a0[p] = first * (1.0 / H)

            def body(i, carry, start=start):
                par = lax.rem(start + i, 2)
                for g in range(G):
                    halo_wait(par, g)
                    sweep(par, g)

                    @pl.when(start + i < OUTER * SWEEPS - 1)
                    def _(g=g):
                        halo_start(1 - par, g)
                return carry

            lax.fori_loop(0, SWEEPS, body, 0)

        par = (OUTER * SWEEPS) % 2
        si_to = (tl * PL) // LP
        at_plane = tl * PL - si_to * LP

        def deliver(a, wait):
            for off in range(T):
                tt = lax.rem(t + T - 1 - off, T)
                out = (state_out, adjoint_out)[a]
                send(
                    raw.at[a, pl.ds(tt * LS, LS)],
                    out.at[:, pl.ds(at_plane, PL), pl.ds(pl.multiple_of(q * R, 8), R)],
                    osend.at[a, off], orecv.at[a, q, tl - si_to * PXS], tt, so * POOL + si_to, wait,
                )

        for a in range(2):
            for p in range(PL):
                fields = [[cur[par, g, 2 * a + i, p] for i in range(2)] for g in range(G)]
                modes = [(fields[0][0], None)] + [tuple(f) for f in fields[1:]]
                modes.append((fields[0][1], None))
                for n, value in enumerate(irfft(modes)):
                    raw[a, n, p] = value * (1.0 / H)
            deliver(a, False)
        for a, out in enumerate((state_out, adjoint_out)):
            for qq in range(PARTS):
                for j in range(PXS):
                    arrived(
                        out.at[:, pl.ds(j * PL, PL), pl.ds(qq * R, R)], orecv.at[a, qq, j]
                    )
            deliver(a, True)

    dma = pltpu.SemaphoreType.DMA
    scratch = [
        pltpu.VMEM((3, H, PL, R, NZ), f32),
        pltpu.VMEM((2, G, 4, PL, R, NZ), f32),
        pltpu.VMEM((2, 2, G, 4, R, NZ), f32),
        pltpu.VMEM((2, 2, G, 4 * PL, NZ), f32),
        pltpu.VMEM((2, 2, G, 4 * PL, NZ), f32),
        pltpu.VMEM((PL + 2, R + 32, NZ), f32),
        pltpu.VMEM((PL, R, NZ), f32),
        pltpu.VMEM((6, PL, R, NZ), f32),
        pltpu.VMEM((PL, R, NZ), f32),
        pltpu.VMEM((G + 1, PL, R, NZ), f32),
        pltpu.VMEM((G, 2, PL, R, NZ), f32),
        pltpu.VMEM((PL, R, NZ), f32),
        pltpu.VMEM((PL, R, NZ), f32),
        dma((3, PARTS, PXS)),
        dma((3, T)),
        dma((2,)),
        dma((2,)),
        dma((2,)),
        dma((2,)),
        dma((2, 4, G)),
        dma((2, 4, G)),
        dma((2, T)),
        dma((2, PARTS, PXS)),
    ]
    return kernel, scratch


def solution(mesh):
    T, S = mesh.shape["tm"], mesh.shape["space"]

    def on_device(state_guess, adjoint_guess, target, initial_state, diffusivity):
        LS, LP, NY, NZ = state_guess.shape
        kernel, scratch = make_kernel(T, S, LS, LP, NY, NZ)
        shape = jax.ShapeDtypeStruct(state_guess.shape, jnp.float32)
        return pl.pallas_call(
            kernel,
            out_shape=(shape, shape),
            in_specs=[pl.BlockSpec(memory_space=pl.ANY)] * 5,
            out_specs=[pl.BlockSpec(memory_space=pl.ANY)] * 2,
            scratch_shapes=scratch,
            compiler_params=pltpu.CompilerParams(collective_id=0, has_side_effects=True),
        )(state_guess, adjoint_guess, target, initial_state, diffusivity)

    field = P("tm", "space", None, None)
    cells = P("space", None, None)
    return jax.shard_map(
        on_device, mesh=mesh, in_specs=(field, field, field, cells, cells),
        out_specs=(field, field), check_vma=False,
    )
```

time: 323 us -> 46.1 us (0.14)
  waiting for transfers between devices: 217 us -> 0 us
  starting transfers between devices: 65.5 us -> 0 us
  Pallas kernels: 0 us -> 42.9 us
  other arithmetic: 35.2 us -> 0 us
    ppermute x30 -> x0, waiting for transfers between devices: 217 us -> none  [the longest x11 126 us: extended(): lax.ppermute(head, axis, [((i + 1) % count, i) for i in range(ends)])]
    ppermute x30 -> x0, starting transfers between devices: 65.5 us -> none  [the longest x11 39.6 us: extended(): lax.ppermute(head, axis, [((i + 1) % count, i) for i in range(ends)])]
    pallas_call x0 -> x1, Pallas kernels: none -> 42.9 us  [on_device(): pl.pallas_call(kernel, out_shape=(shape, shape), in_specs=[pl.BlockSpec(m...]
    concatenate x11 -> x0, other arithmetic: 15.7 us -> none  [extended(): jnp.concatenate([lax.ppermute(tail, axis, [(i, (i + 1) % count) for i in...]
    add x12 -> x0, other arithmetic: 6.52 us -> none  [the longest x6 4.67 us: on_device(): pushed = right_side + step_size * neighbour_sum(sweep_rimmed, weights)]
    select_n x8 -> x0, other arithmetic: 4.69 us -> none  [the longest x4 3.04 us: butterfly_segment(): jnp.where(upper_half, packed + partner, twiddle(partner - packed, cos_par...]
    sub x13 -> x0, other arithmetic: 3.58 us -> none  [the longest x8 1.77 us: twiddle(): packed[0] * cos_part - packed[1] * sin_part]
  transfers between devices with their start and end apart: 30 -> 0, of which waited for: 25 -> 0; matrix products, arithmetic and copies ran while one was open for 1% -> 0% of each run, Pallas kernels for 0% -> 0%
where the time goes in v1:
time: 46.1 us; the launch traced here: 45.9 us
  Pallas kernels  42.9 us (93%)
  local copies, waits for them, and re-layouts  2.34 us (5%)
  between operations  0.65 us (1%)
    pallas_call x1, Pallas kernels, on_device(): pl.pallas_call(kernel, out_shape=(shape, shape), in_specs=[pl.BlockSpec(m...  42.9 us
    unnamed x4, local copies, waits for them, and re-layouts  2.34 us

profile of v1, /device:TPU:16, one launch (start us, length us, event | category | flops | bytes accessed | tf_op | source)
XLA Modules:
  0.0 45.9 jit_solution(16480486887569373836)
XLA Ops:
  0.6 42.9 %shard_map.68 = (f32[2,2,96,128]{3,2,1,0:T(8,128)}, f32[2,2,96,128]{3,2,1,0:T(8,128)}) custom-call(f32[2,2,96,128]{3,2,1,0:T(8,128)} %state_in.1, f32[2,2,96,128]{3,2,1,0:T(8,128)} %adjoint_in.1, f32[2,2,96,128]{3,2,1,0:T(8,128)} %target_in.1, f32[2,96,128]{2,1,0:T(8,128)} %initial_in.1, f32[2,96,128]{2,1,0:T(8,128)} %kappa_in.1), custom_call_target="tpu_custom_call" | custom-call | tf_op jit(solution)/shard_map/pallas_call | solution.py:442
  43.6 0.0 copy-start
  43.6 1.7 %copy.9 = f32[2,2,96,128]{3,2,1,0:T(8,128)} copy(f32[2,2,96,128]{3,2,1,0:T(8,128)} %get-tuple-element.4) | data formatting | bytes 393216
  45.2 0.0 copy-done
  45.2 0.7 %copy.10 = f32[2,2,96,128]{3,2,1,0:T(8,128)} copy(f32[2,2,96,128]{3,2,1,0:T(8,128)S(1)} %copy-done) | data formatting | bytes 393216
Async XLA Ops:
  43.6 1.7 %copy-start = (f32[2,2,96,128]{3,2,1,0:T(8,128)S(1)}, f32[2,2,96,128]{3,2,1,0:T(8,128)}, u32[]{:S(2)}) copy-start(f32[2,2,96,128]{3,2,1,0:T(8,128)} %get-tuple-element.5) | copy-start | bytes 589828

commit v2 on v1

--- a/solution.py
+++ b/solution.py
@@ -107,8 +107,6 @@
             return {"tm": row * PX + tl, "space": so * POOL + col}
 
         kap[...] = jnp.zeros_like(kap)
-        hx[...] = jnp.zeros_like(hx)
-        hy[...] = jnp.zeros_like(hy)
         barrier = pltpu.get_barrier_semaphore()
         members = POOL * T
         mine = si * T + t
@@ -183,6 +181,12 @@
 
         single(False)
         spread(False)
+
+        for d, edges in enumerate((hx, hx, hy, hy)):
+            @pl.when(jnp.logical_not(has[d]))
+            def _(d=d, edges=edges):
+                for par in range(2):
+                    edges[par, d % 2] = jnp.zeros(edges.shape[2:], f32)
 
         arrived(kap.at[pl.ds(1, PL), pl.ds(0, W)], one_recv.at[0])
 
@@ -271,6 +275,11 @@
                 def _(d=d):
                     dst = hx.at[par, d, g] if d < 2 else hy.at[par, d - 2, g]
                     arrived(dst, hrecv.at[par, d, g])
+
+        def halo_sent(par, g):
+            for d in range(4):
+                @pl.when(has[d])
+                def _(d=d):
                     halo_copy(par, d, g).wait_send()
 
         for a in range(2):
@@ -364,6 +373,11 @@
                 par = lax.rem(start + i, 2)
                 for g in range(G):
                     halo_wait(par, g)
+
+                    @pl.when(start + i > 0)
+                    def _(g=g):
+                        halo_sent(1 - par, g)
+
                     sweep(par, g)
 
                     @pl.when(start + i < OUTER * SWEEPS - 1)
@@ -374,12 +388,15 @@
             lax.fori_loop(0, SWEEPS, body, 0)
 
         par = (OUTER * SWEEPS) % 2
+        for g in range(G):
+            halo_sent(1 - par, g)
         si_to = (tl * PL) // LP
         at_plane = tl * PL - si_to * LP
 
         def deliver(a, wait):
             for off in range(T):
-                tt = lax.rem(t + T - 1 - off, T)
+                row, col = (T - 1 - off) // PX, (T - 1 - off) % PX
+                tt = lax.rem(th + row, T // PX) * PX + lax.rem(tl + col, PX)
                 out = (state_out, adjoint_out)[a]
                 send(
                     raw.at[a, pl.ds(tt * LS, LS)],
@@ -393,7 +410,7 @@
                 modes = [(fields[0][0], None)] + [tuple(f) for f in fields[1:]]
                 modes.append((fields[0][1], None))
                 for n, value in enumerate(irfft(modes)):
-                    raw[a, n, p] = value * (1.0 / H)
+                    raw[a, n, p] = value
             deliver(a, False)
         for a, out in enumerate((state_out, adjoint_out)):
             for qq in range(PARTS):
@@ -438,15 +455,15 @@
     def on_device(state_guess, adjoint_guess, target, initial_state, diffusivity):
         LS, LP, NY, NZ = state_guess.shape
         kernel, scratch = make_kernel(T, S, LS, LP, NY, NZ)
-        shape = jax.ShapeDtypeStruct(state_guess.shape, jnp.float32)
-        return pl.pallas_call(
+        outs = pl.pallas_call(
             kernel,
-            out_shape=(shape, shape),
+            out_shape=(pltpu.VMEM(state_guess.shape, jnp.float32),) * 2,
             in_specs=[pl.BlockSpec(memory_space=pl.ANY)] * 5,
-            out_specs=[pl.BlockSpec(memory_space=pl.ANY)] * 2,
+            out_specs=[pl.BlockSpec(memory_space=pltpu.VMEM)] * 2,
             scratch_shapes=scratch,
             compiler_params=pltpu.CompilerParams(collective_id=0, has_side_effects=True),
         )(state_guess, adjoint_guess, target, initial_state, diffusivity)
+        return outs[0] * (1.0 / (T * LS)), outs[1] * (1.0 / (T * LS))
 
     field = P("tm", "space", None, None)
     cells = P("space", None, None)

time: 46.1 us -> 44.4 us (0.963)
  local copies, waits for them, and re-layouts: 2.34 us -> 0 us
  other arithmetic: 0 us -> 0.77 us
    unnamed x4 -> x0, local copies, waits for them, and re-layouts: 2.34 us -> none
    mul x0 -> x1, other arithmetic: none -> 0.77 us  [on_device(): return (outs[0] * (1.0 / (T * LS)), outs[1] * (1.0 / (T * LS)))]
where the time goes in v2:
time: 44.4 us; the launch traced here: 44.3 us
  Pallas kernels  42.8 us (96%)
  other arithmetic  0.77 us (2%)
  between operations  0.64 us (1%)
    pallas_call x1, Pallas kernels, on_device(): pl.pallas_call(kernel, out_shape=(pltpu.VMEM(state_guess.shape, jnp.float...  42.8 us

profile of v2, /device:TPU:16, one launch (start us, length us, event | category | flops | bytes accessed | tf_op | source)
XLA Modules:
  0.0 44.3 jit_solution(1298839104090650969)
XLA Ops:
  0.6 42.8 %shard_map.68 = (f32[2,2,96,128]{3,2,1,0:T(8,128)S(1)}, f32[2,2,96,128]{3,2,1,0:T(8,128)S(1)}) custom-call(f32[2,2,96,128]{3,2,1,0:T(8,128)} %state_in.1, f32[2,2,96,128]{3,2,1,0:T(8,128)} %adjoint_in.1, f32[2,2,96,128]{3,2,1,0:T(8,128)} %target_in.1, f32[2,96,128]{2,1,0:T(8,128)} %initial_in.1, f32[2,96,128]{2,1,0:T(8,128)} %kappa_in.1), custom_call_target="tpu_custom_call" | custom-call | tf_op jit(solution)/shard_map/pallas_call | solution.py:458
  43.5 0.8 %broadcast_multiply_fusion = (f32[2,2,96,128]{3,2,1,0:T(8,128)}, f32[2,2,96,128]{3,2,1,0:T(8,128)}) fusion(f32[2,2,96,128]{3,2,1,0:T(8,128)S(1)} %get-tuple-element.5, f32[2,2,96,128]{3,2,1,0:T(8,128)S(1)} %get-tuple-element.4), kind=kLoop, calls=%fused_computation | loop fusion | flops 98304 | bytes 786432 | tf_op jit(solution)/shard_map/mul | solution.py:466

commit v3 on v2

--- a/solution.py
+++ b/solution.py
@@ -149,7 +149,7 @@
         def arrived(dst, rsem):
             pltpu.make_async_copy(dst, dst, rsem).wait()
 
-        def single(wait):
+        def single(wait, kappa=True, initial=True):
             col = lax.rem(tl, POOL)
             qd = q_of(th, col)
             tt = th * PX + si * PXS + tl // POOL
@@ -157,14 +157,16 @@
             planes = pl.ds((tl // POOL) * PL, PL)
             top = pl.multiple_of(jnp.clip(qd * R - 8, 0, NY - W), 8)
             low = pl.multiple_of(top - qd * R + 16, 8)
-            send(
-                kappa_in.at[planes, pl.ds(top, W)], kap.at[pl.ds(1, PL), pl.ds(low, W)],
-                one_send.at[0], one_recv.at[0], tt, ss, wait,
-            )
-            send(
-                initial_in.at[planes, pl.ds(pl.multiple_of(qd * R, 8), R)], ini,
-                one_send.at[1], one_recv.at[1], tt, ss, wait,
-            )
+            if kappa:
+                send(
+                    kappa_in.at[planes, pl.ds(top, W)], kap.at[pl.ds(1, PL), pl.ds(low, W)],
+                    one_send.at[0], one_recv.at[0], tt, ss, wait,
+                )
+            if initial:
+                send(
+                    initial_in.at[planes, pl.ds(pl.multiple_of(qd * R, 8), R)], ini,
+                    one_send.at[1], one_recv.at[1], tt, ss, wait,
+                )
 
         def spread(wait):
             for a, source in enumerate((state_in, adjoint_in, target_in)):
@@ -179,8 +181,9 @@
                             a2a_send.at[a, off, j], a2a_recv.at[a, t], tt, so * POOL + col, wait,
                         )
 
-        single(False)
+        single(False, initial=False)
         spread(False)
+        single(False, kappa=False)
 
         for d, edges in enumerate((hx, hx, hy, hy)):
             @pl.when(jnp.logical_not(has[d]))
@@ -292,16 +295,16 @@
                         rows_out(0, g, 2 * a + i, p, pair[i])
         for g in range(G):
             halo_start(0, g)
-        arrived(ini, one_recv.at[1])
-        for p in range(PL):
-            fs[p] = ini[p] - raw[0, H - 1, p]
-            a0[p] = raw[1, 0, p]
         gather(2)
         for p in range(PL):
             pairs = paired(rfft([raw[2, n, p] for n in range(H)]))
             for g, pair in enumerate(pairs):
                 for i in range(2):
                     that[g, i, p] = -TAU * pair[i]
+        arrived(ini, one_recv.at[1])
+        for p in range(PL):
+            fs[p] = ini[p] - raw[0, H - 1, p]
+            a0[p] = raw[1, 0, p]
         single(True)
         spread(True)
 

time: 44.4 us -> 44.2 us (level)
  no operation moved by 1% of the time
where the time goes in v3:
time: 44.2 us; the launch traced here: 44 us
  Pallas kernels  42.6 us (96%)
  other arithmetic  0.77 us (2%)
  between operations  0.64 us (1%)
    pallas_call x1, Pallas kernels, on_device(): pl.pallas_call(kernel, out_shape=(pltpu.VMEM(state_guess.shape, jnp.float...  42.6 us

profile of v3, /device:TPU:16, one launch (start us, length us, event | category | flops | bytes accessed | tf_op | source)
XLA Modules:
  0.0 44.0 jit_solution(2211972904444564024)
XLA Ops:
  0.6 42.6 %shard_map.68 = (f32[2,2,96,128]{3,2,1,0:T(8,128)S(1)}, f32[2,2,96,128]{3,2,1,0:T(8,128)S(1)}) custom-call(f32[2,2,96,128]{3,2,1,0:T(8,128)} %state_in.1, f32[2,2,96,128]{3,2,1,0:T(8,128)} %adjoint_in.1, f32[2,2,96,128]{3,2,1,0:T(8,128)} %target_in.1, f32[2,96,128]{2,1,0:T(8,128)} %initial_in.1, f32[2,96,128]{2,1,0:T(8,128)} %kappa_in.1), custom_call_target="tpu_custom_call" | custom-call | tf_op jit(solution)/shard_map/pallas_call | solution.py:461
  43.3 0.8 %broadcast_multiply_fusion = (f32[2,2,96,128]{3,2,1,0:T(8,128)}, f32[2,2,96,128]{3,2,1,0:T(8,128)}) fusion(f32[2,2,96,128]{3,2,1,0:T(8,128)S(1)} %get-tuple-element.5, f32[2,2,96,128]{3,2,1,0:T(8,128)S(1)} %get-tuple-element.4), kind=kLoop, calls=%fused_computation | loop fusion | flops 98304 | bytes 786432 | tf_op jit(solution)/shard_map/mul | solution.py:469
